TPU v7x, 32 devices: a whole 2x2x4 slice. The times are simulated.
32 devices in a mesh: group: 4 (over x, core), ctx: 8 (over z, y).
Axes of the slice: x: 2, y: 2, z: 4, core: 2. Of those that a mesh axis runs over, the one named last changes fastest.
Arguments:
- query_rows: bfloat16 [4, 2048, 4096], P('group', 'ctx'), may hold values from -250 to 250
- key_rows: bfloat16 [4, 2048, 512], P('group', 'ctx'), may hold values from -7 to 7
- value_rows: bfloat16 [4, 2048, 512], P('group', 'ctx'), may hold values from -6 to 6
- documents: int32 [4, 2048], P('group', 'ctx'), may hold values from 0 to 3, never falling along the last dimension, each value on 1 to 1280 neighbouring positions
- owners: int32 [4, 64, 1], P('group', 'ctx'), may hold values from 0 to 3; in each aligned block of 8 rows (0 to 7, 8 to 15, ..., all dimensions but the last counted through in order) at most 2 rows name the same one
Outputs:
- attended: bfloat16 [4, 2048, 4096], P('group', 'ctx')
- page_pool: bfloat16 [4, 64, 2, 128, 128], P('group', 'ctx')
- page_scales: bfloat16 [4, 64, 2], P('group', 'ctx')
Inputs may be any that keep to these rules, and one draw needn't show every extreme that they name: `documents`: document numbers never fall along a group's tokens; each document has at most 1280 tokens. `owners`: among the pages of one device, no owner is named more than 2 times.
All inputs are finite; a program needn't handle non-finite values.
Results may differ from a plain program's by a relative error of at most 0.0028.
Values may be sent and summed in bfloat16 or wider, within the bound.
A program may use at most 128 MiB of HBM per device.

v0:
```python
import math
import jax
import jax.numpy as jnp
from jax import lax
from jax.sharding import PartitionSpec as P

E = 128
HQ = 32
HK = 4
PAGE = 128
epsilon = 1e-06
masked_score = -1e30


def split_heads(queries_here, keys_here, values_here, doc_marks):
    tokens = queries_here.shape[0]
    ctx_count = lax.axis_size("ctx")
    per_device = HQ // ctx_count
    score_scale = 1.0 / math.sqrt(E)
    kv_pairs = jnp.stack(
        [keys_here.reshape(tokens, HK, E), values_here.reshape(tokens, HK, E)], axis=2
    )
    spread = jnp.repeat(kv_pairs, ctx_count // HK, axis=1)
    spread_marks = jnp.broadcast_to(doc_marks[:, None], (tokens, ctx_count))
    all_pairs, all_marks = (
        lax.all_to_all(spread, "ctx", split_axis=1, concat_axis=0, tiled=True),
        lax.all_to_all(spread_marks, "ctx", split_axis=1, concat_axis=0, tiled=True),
    )
    key_all = all_pairs[:, 0, 0]
    value_all = all_pairs[:, 0, 1]
    marks_all = all_marks[:, 0]
    length = key_all.shape[0]
    key_pos = jnp.arange(length, dtype=jnp.int32)
    block_rows = math.gcd(length, 512)
    shaped = queries_here.reshape(tokens, ctx_count, per_device, E)
    head_rows = lax.all_to_all(shaped, "ctx", split_axis=1, concat_axis=0, tiled=True)[:, 0]
    head_count = head_rows.shape[1]

    def one_block(block_index):
        first_row = block_index * block_rows
        query_block = lax.dynamic_slice_in_dim(head_rows, first_row, block_rows, 0)
        mark_rows = lax.dynamic_slice_in_dim(marks_all, first_row, block_rows, 0)
        query_pos = first_row + jnp.arange(block_rows, dtype=jnp.int32)
        scores = (
            jnp.einsum("qhe,ke->hqk", query_block, key_all, preferred_element_type=jnp.float32)
            * score_scale
        )
        visible = (mark_rows[:, None] == marks_all[None, :]) & (
            query_pos[:, None] >= key_pos[None, :]
        )
        scores = jnp.where(visible, scores, masked_score)
        largest = jnp.max(scores, axis=-1, keepdims=True)
        weights = jnp.exp(scores - largest)
        totals = jnp.sum(weights, axis=-1)
        weighted = jnp.einsum(
            "hqk,ke->qhe",
            weights.astype(jnp.bfloat16),
            value_all,
            preferred_element_type=jnp.float32,
        )
        return (weighted / jnp.transpose(totals)[..., None]).astype(jnp.bfloat16)

    blocks = lax.map(one_block, jnp.arange(length // block_rows, dtype=jnp.int32))
    result = blocks.reshape(length, 1, head_count, E)
    merged = lax.all_to_all(result, "ctx", split_axis=0, concat_axis=1, tiled=True)
    return merged.reshape(tokens, HQ * E)


def deliver_pages(keys_here, values_here, owner_list):
    tokens = keys_here.shape[0]
    block_count = tokens // PAGE
    key_pages = keys_here.reshape(block_count, PAGE, HK, E).transpose(0, 2, 1, 3)
    value_pages = values_here.reshape(block_count, PAGE, HK, E).transpose(0, 2, 1, 3)
    page_count = block_count * HK
    kv_pairs = jnp.stack([key_pages, value_pages], axis=2).reshape(page_count, 2, PAGE, E)
    magnitude = jnp.max(jnp.abs(kv_pairs.astype(jnp.float32)), axis=(2, 3)) + epsilon
    scales = magnitude.astype(jnp.bfloat16)
    stored = (kv_pairs.astype(jnp.float32) / scales.astype(jnp.float32)[:, :, None, None]).astype(
        jnp.bfloat16
    )
    groups_n = lax.axis_size("group")
    slot_depth = max(2, (page_count + groups_n - 1) // groups_n)
    page_order = jnp.arange(page_count, dtype=jnp.int32)
    earlier = (owner_list[:, None] == owner_list[None, :]) & (
        page_order[None, :] < page_order[:, None]
    )
    page_rank = jnp.sum(earlier.astype(jnp.int32), axis=1)
    slot_of = owner_list * slot_depth + page_rank
    select = (
        jnp.arange(groups_n * slot_depth, dtype=jnp.int32)[:, None] == slot_of[None, :]
    ).astype(jnp.bfloat16)
    packed = jnp.dot(
        select, stored.reshape(page_count, 2 * PAGE * E), preferred_element_type=jnp.float32
    ).astype(jnp.bfloat16)
    packed_scales = jnp.dot(select, scales, preferred_element_type=jnp.float32).astype(jnp.bfloat16)
    packed = packed.reshape(groups_n, slot_depth, 2, PAGE, E)
    packed_scales = packed_scales.reshape(groups_n, slot_depth, 2)
    arrived, arrived_scales = (
        lax.all_to_all(packed, "group", split_axis=0, concat_axis=0, tiled=True),
        lax.all_to_all(packed_scales, "group", split_axis=0, concat_axis=0, tiled=True),
    )
    return (
        arrived.reshape(1, groups_n * slot_depth, 2, PAGE, E),
        arrived_scales.reshape(1, groups_n * slot_depth, 2),
    )


def local(query_rows, key_rows, value_rows, documents, owners):
    queries_here = query_rows[0]
    keys_here = key_rows[0]
    values_here = value_rows[0]
    doc_marks = documents[0].astype(jnp.bfloat16)
    attended = split_heads(queries_here, keys_here, values_here, doc_marks)
    page_pool, page_scales = deliver_pages(keys_here, values_here, owners[0, :, 0])
    return (attended[None], page_pool, page_scales)


def solution(mesh):
    placed = (
        P("group", "ctx", None),
        P("group", "ctx", None),
        P("group", "ctx", None),
        P("group", "ctx"),
        P("group", "ctx", None),
    )
    return jax.shard_map(
        local,
        mesh=mesh,
        in_specs=placed,
        out_specs=(
            P("group", "ctx", None),
            P("group", "ctx", None, None, None),
            P("group", "ctx", None),
        ),
        check_vma=False,
    )
```

profile of v0, /device:TPU:0, one launch (start us, length us, event | category | flops | bytes accessed | tf_op | source)
XLA Modules:
  0.0 243.0 jit_solution(9955925464402207372)
XLA Ops:
  0.6 0.7 convert_reduce_fusion.1
  1.9 0.7 reduce.5
  2.5 0.6 reshape.89
  3.1 7.3 %all-to-all-start = ((bf16[8,2,128]{2,1,0:T(2,128)(2,1)}), bf16[8,2,128]{2,1,0:T(2,128)(2,1)S(1)}, u32[]{:S(2)}, u32[]{:S(2)}) async-start(bf16[8,2,128]{2,1,0:T(2,128)(2,1)} %reshape.89), calls=%async_computation | async-start | bytes 8192 | tf_op jit(solution)/shard_map/all_to_all | solution.py:27
  10.4 1.0 stack_reshape_squeeze.7
  11.5 1.0 stack_reshape_squeeze.6
  12.9 3.9 %all-to-all-done = bf16[8,2,128]{2,1,0:T(2,128)(2,1)S(1)} async-done(((bf16[8,2,128]{2,1,0:T(2,128)(2,1)}), bf16[8,2,128]{2,1,0:T(2,128)(2,1)S(1)}, u32[]{:S(2)}, u32[]{:S(2)}) %all-to-all-start) | async-done | bytes 4128 | tf_op jit(solution)/shard_map/all_to_all | solution.py:27
  16.9 1.2 broadcast_in_dim.25
  18.0 3.6 %all-to-all-start.2 = ((bf16[256,8,2,128]{3,0,2,1:T(8,128)(2,1)}), bf16[256,8,2,128]{3,0,2,1:T(8,128)(2,1)S(1)}, u32[]{:S(2)}, u32[]{:S(2)}) async-start(bf16[256,8,2,128]{3,0,2,1:T(8,128)(2,1)} %bitcast.6), calls=%async_computation.2 | async-start | bytes 2097152 | tf_op jit(solution)/shard_map/all_to_all | solution.py:26
  21.6 3.3 %copy.47 = bf16[1,256,4096]{1,2,0:T(8,128)(2,1)S(1)} copy(bf16[1,256,4096]{2,1,0:T(8,128)(2,1)} %param.7) | data formatting | bytes 4194304 | tf_op args[0]
  24.9 2.4 copy.48
  27.3 19.0 %all-to-all-done.2 = bf16[256,8,2,128]{3,0,2,1:T(8,128)(2,1)S(1)} async-done(((bf16[256,8,2,128]{3,0,2,1:T(8,128)(2,1)}), bf16[256,8,2,128]{3,0,2,1:T(8,128)(2,1)S(1)}, u32[]{:S(2)}, u32[]{:S(2)}) %all-to-all-start.2) | async-done | bytes 1048608 | tf_op jit(solution)/shard_map/all_to_all | solution.py:26
  46.3 3.6 %all-to-all-start.1 = ((bf16[256,8,4,128]{3,0,2,1:T(8,128)(2,1)}), bf16[256,8,4,128]{3,0,2,1:T(8,128)(2,1)S(1)}, u32[]{:S(2)}, u32[]{:S(2)}) async-start(bf16[256,8,4,128]{3,0,2,1:T(8,128)(2,1)} %copy.48), calls=%async_computation.1 | async-start | bytes 4194304 | tf_op jit(solution)/shard_map/all_to_all | solution.py:36
  50.0 0.8 reshape_squeeze.11
  50.7 1.0 reshape_squeeze.10
  51.7 1.0 copy.57
  53.9 0.9 copy.66
  55.7 0.9 slice_bitcast_fusion
  56.6 41.6 %all-to-all-done.1 = bf16[256,8,4,128]{3,0,2,1:T(8,128)(2,1)S(1)} async-done(((bf16[256,8,4,128]{3,0,2,1:T(8,128)(2,1)}), bf16[256,8,4,128]{3,0,2,1:T(8,128)(2,1)S(1)}, u32[]{:S(2)}, u32[]{:S(2)}) %all-to-all-start.1) | async-done | bytes 2097184 | tf_op jit(solution)/shard_map/all_to_all | solution.py:36
  98.2 3.2 %all-to-all-start.5 = ((bf16[4,2,2]{1,2,0:T(2,128)(2,1)}), bf16[4,2,2]{1,2,0:T(2,128)(2,1)S(1)}, u32[]{:S(2)}, u32[]{:S(2)}) async-start(bf16[4,2,2]{1,2,0:T(2,128)(2,1)} %copy.59), calls=%async_computation.5 | async-start | bytes 4096 | tf_op jit(solution)/shard_map/all_to_all | solution.py:100
  101.4 1.5 copy.49
  102.9 2.2 all-to-all-done.5
  105.1 3.5 %all-to-all-start.4 = ((bf16[4,2,2,128,128]{4,3,2,1,0:T(8,128)(2,1)}), bf16[4,2,2,128,128]{4,3,2,1,0:T(8,128)(2,1)S(1)}, u32[]{:S(2)}, u32[]{:S(2)}) async-start(bf16[4,2,2,128,128]{4,3,2,1,0:T(8,128)(2,1)} %bitcast.44), calls=%async_computation.4 | async-start | bytes 1048576 | tf_op jit(solution)/shard_map/all_to_all | solution.py:99
  108.6 68.9 %while.11 = (s32[]{:T(128)}, bf16[4,512,4,128]{3,1,0,2:T(8,128)(2,1)}, s32[4]{0:T(128)S(1)}, bf16[2048]{0:T(1024)(128)(2,1)S(1)}, bf16[2048,1]{0,1:T(2,128)(2,1)...) while((s32[]{:T(128)}, ...), condition=%wide.region_3.4_spmd.clone, body=%wide.region_0.3_spmd.clone.sunk | while | flops 2199384576 | bytes 56683728 | solution.py:63
  110.0 1.2 fusion.44
  111.2 4.8 %bitcast_reduce_fusion.3 = (f32[4,512]{1,0:T(4,128)S(1)}, f32[512,4,2048]{2,0,1:T(8,128)S(1)}) fusion(pred[512,2048]{1,0:T(8,128)(4,1)S(1)} %fusion.44, bf16[2048,128]{1,0:T(8,128)(2,1)} %get-tuple-element.186, bf16[2048,4,128]{2,0,1:T(8,128)(2,1)} %get-tuple-element.185, s32[]{:T(128)S(6)} %select_n.39), kind=kOutput, calls=%fused_computation.2.clone.1 | convolution fusion | flops 1086322688 | bytes 18882564 | tf_op jit(solution)/shard_map/while/body/eval_jaxpr/qhe,ke->hqk/dot_general | solution.py:45
  115.9 4.5 %fusion.45 = f32[4,512]{1,0:T(4,128)S(1)} fusion(f32[512,4,2048]{2,0,1:T(8,128)S(1)} %get-tuple-element.152, f32[4,512]{1,0:T(4,128)S(1)} %get-tuple-element.153, pred[512,2048]{1,0:T(8,128)(4,1)S(1)} %fusion.44), kind=kLoop, calls=%fused_computation.5.clone.1 | loop fusion | flops 16775168 | bytes 17842176 | tf_op jit(solution)/shard_map/while/body/eval_jaxpr/reduce_sum | solution.py:54
  120.4 5.4 %fusion.46 = bf16[4,512,4,128]{3,1,0,2:T(8,128)(2,1)} fusion(bf16[4,512,4,128]{3,1,0,2:T(8,128)(2,1)} %get-tuple-element.168, s32[]{:T(128)S(6)} %copy.74, f32[512,4,2048]{2,0,1:T(8,128)S(1)} %get-tuple-element.152, f32[4,512]{1,0:T(4,128)S(1)} %get-tuple-element.153, pred[512,2048]{1,0:T(8,128)(4,1)S(1)} %fusion.44, ...), kind=kOutput, calls=%fused_computation.14.clone.1 | convolution fusion | flops 1091043328 | bytes 18890756 | tf_op jit(solution)/shard_map/while/body/eval_jaxpr/hqk,ke->qhe/dot_general | solution.py:55
  127.2 1.2 fusion.44
  128.4 4.8 %bitcast_reduce_fusion.3 = (f32[4,512]{1,0:T(4,128)S(1)}, f32[512,4,2048]{2,0,1:T(8,128)S(1)}) fusion(pred[512,2048]{1,0:T(8,128)(4,1)S(1)} %fusion.44, bf16[2048,128]{1,0:T(8,128)(2,1)} %get-tuple-element.186, bf16[2048,4,128]{2,0,1:T(8,128)(2,1)} %get-tuple-element.185, s32[]{:T(128)S(6)} %select_n.39), kind=kOutput, calls=%fused_computation.2.clone.1 | convolution fusion | flops 1086322688 | bytes 18882564 | tf_op jit(solution)/shard_map/while/body/eval_jaxpr/qhe,ke->hqk/dot_general | solution.py:45
  133.1 4.5 %fusion.45 = f32[4,512]{1,0:T(4,128)S(1)} fusion(f32[512,4,2048]{2,0,1:T(8,128)S(1)} %get-tuple-element.152, f32[4,512]{1,0:T(4,128)S(1)} %get-tuple-element.153, pred[512,2048]{1,0:T(8,128)(4,1)S(1)} %fusion.44), kind=kLoop, calls=%fused_computation.5.clone.1 | loop fusion | flops 16775168 | bytes 17842176 | tf_op jit(solution)/shard_map/while/body/eval_jaxpr/reduce_sum | solution.py:54
  137.6 5.4 %fusion.46 = bf16[4,512,4,128]{3,1,0,2:T(8,128)(2,1)} fusion(bf16[4,512,4,128]{3,1,0,2:T(8,128)(2,1)} %get-tuple-element.168, s32[]{:T(128)S(6)} %copy.74, f32[512,4,2048]{2,0,1:T(8,128)S(1)} %get-tuple-element.152, f32[4,512]{1,0:T(4,128)S(1)} %get-tuple-element.153, pred[512,2048]{1,0:T(8,128)(4,1)S(1)} %fusion.44, ...), kind=kOutput, calls=%fused_computation.14.clone.1 | convolution fusion | flops 1091043328 | bytes 18890756 | tf_op jit(solution)/shard_map/while/body/eval_jaxpr/hqk,ke->qhe/dot_general | solution.py:55
  144.4 1.2 fusion.44
  145.6 4.8 %bitcast_reduce_fusion.3 = (f32[4,512]{1,0:T(4,128)S(1)}, f32[512,4,2048]{2,0,1:T(8,128)S(1)}) fusion(pred[512,2048]{1,0:T(8,128)(4,1)S(1)} %fusion.44, bf16[2048,128]{1,0:T(8,128)(2,1)} %get-tuple-element.186, bf16[2048,4,128]{2,0,1:T(8,128)(2,1)} %get-tuple-element.185, s32[]{:T(128)S(6)} %select_n.39), kind=kOutput, calls=%fused_computation.2.clone.1 | convolution fusion | flops 1086322688 | bytes 18882564 | tf_op jit(solution)/shard_map/while/body/eval_jaxpr/qhe,ke->hqk/dot_general | solution.py:45
  150.4 4.5 %fusion.45 = f32[4,512]{1,0:T(4,128)S(1)} fusion(f32[512,4,2048]{2,0,1:T(8,128)S(1)} %get-tuple-element.152, f32[4,512]{1,0:T(4,128)S(1)} %get-tuple-element.153, pred[512,2048]{1,0:T(8,128)(4,1)S(1)} %fusion.44), kind=kLoop, calls=%fused_computation.5.clone.1 | loop fusion | flops 16775168 | bytes 17842176 | tf_op jit(solution)/shard_map/while/body/eval_jaxpr/reduce_sum | solution.py:54
  154.8 5.4 %fusion.46 = bf16[4,512,4,128]{3,1,0,2:T(8,128)(2,1)} fusion(bf16[4,512,4,128]{3,1,0,2:T(8,128)(2,1)} %get-tuple-element.168, s32[]{:T(128)S(6)} %copy.74, f32[512,4,2048]{2,0,1:T(8,128)S(1)} %get-tuple-element.152, f32[4,512]{1,0:T(4,128)S(1)} %get-tuple-element.153, pred[512,2048]{1,0:T(8,128)(4,1)S(1)} %fusion.44, ...), kind=kOutput, calls=%fused_computation.14.clone.1 | convolution fusion | flops 1091043328 | bytes 18890756 | tf_op jit(solution)/shard_map/while/body/eval_jaxpr/hqk,ke->qhe/dot_general | solution.py:55
  161.6 1.2 fusion.44
  162.8 4.8 %bitcast_reduce_fusion.3 = (f32[4,512]{1,0:T(4,128)S(1)}, f32[512,4,2048]{2,0,1:T(8,128)S(1)}) fusion(pred[512,2048]{1,0:T(8,128)(4,1)S(1)} %fusion.44, bf16[2048,128]{1,0:T(8,128)(2,1)} %get-tuple-element.186, bf16[2048,4,128]{2,0,1:T(8,128)(2,1)} %get-tuple-element.185, s32[]{:T(128)S(6)} %select_n.39), kind=kOutput, calls=%fused_computation.2.clone.1 | convolution fusion | flops 1086322688 | bytes 18882564 | tf_op jit(solution)/shard_map/while/body/eval_jaxpr/qhe,ke->hqk/dot_general | solution.py:45
  167.6 4.5 %fusion.45 = f32[4,512]{1,0:T(4,128)S(1)} fusion(f32[512,4,2048]{2,0,1:T(8,128)S(1)} %get-tuple-element.152, f32[4,512]{1,0:T(4,128)S(1)} %get-tuple-element.153, pred[512,2048]{1,0:T(8,128)(4,1)S(1)} %fusion.44), kind=kLoop, calls=%fused_computation.5.clone.1 | loop fusion | flops 16775168 | bytes 17842176 | tf_op jit(solution)/shard_map/while/body/eval_jaxpr/reduce_sum | solution.py:54
  172.1 5.4 %fusion.46 = bf16[4,512,4,128]{3,1,0,2:T(8,128)(2,1)} fusion(bf16[4,512,4,128]{3,1,0,2:T(8,128)(2,1)} %get-tuple-element.168, s32[]{:T(128)S(6)} %copy.74, f32[512,4,2048]{2,0,1:T(8,128)S(1)} %get-tuple-element.152, f32[4,512]{1,0:T(4,128)S(1)} %get-tuple-element.153, pred[512,2048]{1,0:T(8,128)(4,1)S(1)} %fusion.44, ...), kind=kOutput, calls=%fused_computation.14.clone.1 | convolution fusion | flops 1091043328 | bytes 18890756 | tf_op jit(solution)/shard_map/while/body/eval_jaxpr/hqk,ke->qhe/dot_general | solution.py:55
  177.5 4.7 %copy.53 = bf16[2048,1,4,128]{3,2,1,0:T(4,128)(2,1)} copy(bf16[2048,1,4,128]{3,0,2,1:T(8,128)(2,1)} %bitcast.120) | data formatting | bytes 4194304 | tf_op jit(solution)/shard_map/reshape | solution.py:64
  182.2 3.6 %all-to-all-start.3 = ((bf16[2048,1,4,128]{3,2,1,0:T(4,128)(2,1)}), bf16[2048,1,4,128]{3,2,1,0:T(4,128)(2,1)S(1)}, u32[]{:S(2)}, u32[]{:S(2)}) async-start(bf16[2048,1,4,128]{3,2,1,0:T(4,128)(2,1)} %copy.53), calls=%async_computation.3 | async-start | bytes 4194304 | tf_op jit(solution)/shard_map/all_to_all | solution.py:65
  185.8 0.6 reshape.83
  186.4 48.4 %all-to-all-done.3 = bf16[2048,1,4,128]{3,2,1,0:T(4,128)(2,1)S(1)} async-done(((bf16[2048,1,4,128]{3,2,1,0:T(4,128)(2,1)}), bf16[2048,1,4,128]{3,2,1,0:T(4,128)(2,1)S(1)}, u32[]{:S(2)}, u32[]{:S(2)}) %all-to-all-start.3) | async-done | bytes 2097184 | tf_op jit(solution)/shard_map/all_to_all | solution.py:65
  234.9 1.6 copy.54
  236.4 2.9 %copy.55 = bf16[256,8,1,4,128]{0,4,3,1,2:T(8,128)(2,1)S(1)} copy(bf16[256,8,1,4,128]{4,0,1,3,2:T(8,128)(2,1)} %bitcast.111) | data formatting | bytes 4194304 | tf_op jit(solution)/shard_map/all_to_all | solution.py:65
  239.3 2.9 %copy.61 = bf16[1,256,4096]{2,1,0:T(8,128)(2,1)} copy(bf16[1,256,4096]{1,2,0:T(8,128)(2,1)S(1)} %bitcast.112) | data formatting | bytes 4194304
  242.2 0.8 copy.79
  (43 shorter events, 5.8 us)
Async XLA Ops:
  3.1 13.7 %all-to-all-start = ((bf16[8,2,128]{2,1,0:T(2,128)(2,1)}), bf16[8,2,128]{2,1,0:T(2,128)(2,1)S(1)}, u32[]{:S(2)}, u32[]{:S(2)}) async-start(bf16[8,2,128]{2,1,0:T(2,128)(2,1)} %reshape.89), calls=%async_computation | async-start | bytes 8192 | tf_op jit(solution)/shard_map/all_to_all | solution.py:27
  18.0 28.3 %all-to-all-start.2 = ((bf16[256,8,2,128]{3,0,2,1:T(8,128)(2,1)}), bf16[256,8,2,128]{3,0,2,1:T(8,128)(2,1)S(1)}, u32[]{:S(2)}, u32[]{:S(2)}) async-start(bf16[256,8,2,128]{3,0,2,1:T(8,128)(2,1)} %bitcast.6), calls=%async_computation.2 | async-start | bytes 2097152 | tf_op jit(solution)/shard_map/all_to_all | solution.py:26
  24.9 25.1 %copy-start = (bf16[1,256,512]{2,1,0:T(8,128)(2,1)S(1)}, bf16[1,256,512]{2,1,0:T(8,128)(2,1)}, u32[]{:S(2)}) copy-start(bf16[1,256,512]{2,1,0:T(8,128)(2,1)} %param.9) | copy-start | bytes 786436
  27.3 26.0 %copy-start.1 = (s32[1,8,1]{1,2,0:T(1,128)S(1)}, s32[1,8,1]{1,2,0:T(1,128)}, u32[]{:S(2)}) copy-start(s32[1,8,1]{1,2,0:T(1,128)} %param.11) | copy-start | bytes 100
  46.3 51.9 %all-to-all-start.1 = ((bf16[256,8,4,128]{3,0,2,1:T(8,128)(2,1)}), bf16[256,8,4,128]{3,0,2,1:T(8,128)(2,1)S(1)}, u32[]{:S(2)}, u32[]{:S(2)}) async-start(bf16[256,8,4,128]{3,0,2,1:T(8,128)(2,1)} %copy.48), calls=%async_computation.1 | async-start | bytes 4194304 | tf_op jit(solution)/shard_map/all_to_all | solution.py:36
  98.2 6.9 %all-to-all-start.5 = ((bf16[4,2,2]{1,2,0:T(2,128)(2,1)}), bf16[4,2,2]{1,2,0:T(2,128)(2,1)S(1)}, u32[]{:S(2)}, u32[]{:S(2)}) async-start(bf16[4,2,2]{1,2,0:T(2,128)(2,1)} %copy.59), calls=%async_computation.5 | async-start | bytes 4096 | tf_op jit(solution)/shard_map/all_to_all | solution.py:100
  105.1 77.1 %all-to-all-start.4 = ((bf16[4,2,2,128,128]{4,3,2,1,0:T(8,128)(2,1)}), bf16[4,2,2,128,128]{4,3,2,1,0:T(8,128)(2,1)S(1)}, u32[]{:S(2)}, u32[]{:S(2)}) async-start(bf16[4,2,2,128,128]{4,3,2,1,0:T(8,128)(2,1)} %bitcast.44), calls=%async_computation.4 | async-start | bytes 1048576 | tf_op jit(solution)/shard_map/all_to_all | solution.py:99
  182.2 52.7 %all-to-all-start.3 = ((bf16[2048,1,4,128]{3,2,1,0:T(4,128)(2,1)}), bf16[2048,1,4,128]{3,2,1,0:T(4,128)(2,1)S(1)}, u32[]{:S(2)}, u32[]{:S(2)}) async-start(bf16[2048,1,4,128]{3,2,1,0:T(4,128)(2,1)} %copy.53), calls=%async_computation.3 | async-start | bytes 4194304 | tf_op jit(solution)/shard_map/all_to_all | solution.py:65
where the time goes:
time: 244 us; the launch traced here: 243 us
  waiting for transfers between devices  115 us (47%)
  matrix products  41.3 us (17%)
  local copies, waits for them, and re-layouts  33.1 us (14%)
  other arithmetic  25.2 us (10%)
  starting transfers between devices  24.7 us (10%)
  loops' own time  2.64 us (1%)
    all_to_all x1, waiting for transfers between devices, split_heads(): lax.all_to_all(result, 'ctx', split_axis=0, concat_axis=1, tiled=True)  48.4 us
    all_to_all x1, waiting for transfers between devices, split_heads(): lax.all_to_all(shaped, 'ctx', split_axis=1, concat_axis=0, tiled=True)[:, 0]  41.6 us
    dot_general x4, matrix products, one_block(): jnp.einsum('hqk,ke->qhe', weights.astype(jnp.bfloat16), value_all, prefer...  21.7 us
    dot_general x4, matrix products, one_block(): jnp.einsum('qhe,ke->hqk', query_block, key_all, preferred_element_type=jn...  19 us
    all_to_all x1, waiting for transfers between devices, split_heads(): lax.all_to_all(spread, 'ctx', split_axis=1, concat_axis=0, tiled=True)  19 us
    reduce_sum x4, other arithmetic, one_block(): totals = jnp.sum(weights, axis=-1)  17.9 us
    unnamed x13, local copies, waits for them, and re-layouts  8.97 us
    all_to_all x1, starting transfers between devices, split_heads(): lax.all_to_all(spread_marks, 'ctx', split_axis=1, concat_axis=0, tiled=True)  7.31 us
  transfers between devices with their start and end apart: 6, of which 5 were waited for; matrix products, arithmetic and copies ran while one was open for 36% of the time, Pallas kernels for 0%

commit v1 on v0

--- a/solution.py
+++ b/solution.py
@@ -62,7 +62,19 @@
 
     blocks = lax.map(one_block, jnp.arange(length // block_rows, dtype=jnp.int32))
     result = blocks.reshape(length, 1, head_count, E)
-    merged = lax.all_to_all(result, "ctx", split_axis=0, concat_axis=1, tiled=True)
+
+    def regions_fit(array_dim, axis_no, view):
+        return jnp.concatenate(
+            lax.all_to_all(
+                jnp.stack(jnp.split(view, lax.axis_size("ctx"), axis=axis_no), axis=0),
+                "ctx",
+                split_axis=0,
+                concat_axis=0,
+            ),
+            axis=array_dim,
+        )
+
+    merged = regions_fit(1, 0, result)
     return merged.reshape(tokens, HQ * E)
 
 

time: 244 us -> 250 us (1.025)
  local copies, waits for them, and re-layouts: 33.1 us -> 36.3 us
  waiting for transfers between devices: 115 us -> 118 us
    unnamed x13 -> x22, local copies, waits for them, and re-layouts: 8.97 us -> 18.4 us
    all_to_all x1, waiting for transfers between devices: 0.01 us -> 5.47 us  [deliver_pages(): lax.all_to_all(packed, 'group', split_axis=0, concat_axis=0, tiled=True)]
    all_to_all x2 -> x0, local copies, waits for them, and re-layouts: 4.45 us -> none  [split_heads(): lax.all_to_all(result, 'ctx', split_axis=0, concat_axis=1, tiled=True)]
where the time goes in v1:
time: 250 us; the launch traced here: 248 us
  waiting for transfers between devices  118 us (47%)
  matrix products  40.5 us (16%)
  local copies, waits for them, and re-layouts  36.3 us (15%)
  other arithmetic  25.2 us (10%)
  starting transfers between devices  24.7 us (10%)
  loops' own time  2.55 us (1%)
    all_to_all x1, waiting for transfers between devices, regions_fit(): lax.all_to_all(jnp.stack(jnp.split(view, lax.axis_size('ctx'), axis=axis_...  47.5 us
    all_to_all x1, waiting for transfers between devices, split_heads(): lax.all_to_all(shaped, 'ctx', split_axis=1, concat_axis=0, tiled=True)[:, 0]  42.4 us
    dot_general x4, matrix products, one_block(): jnp.einsum('hqk,ke->qhe', weights.astype(jnp.bfloat16), value_all, prefer...  21.7 us
    all_to_all x1, waiting for transfers between devices, split_heads(): lax.all_to_all(spread, 'ctx', split_axis=1, concat_axis=0, tiled=True)  19 us
    unnamed x22, local copies, waits for them, and re-layouts  18.4 us
    dot_general x4, matrix products, one_block(): jnp.einsum('qhe,ke->hqk', query_block, key_all, preferred_element_type=jn...  18.3 us
    reduce_sum x4, other arithmetic, one_block(): totals = jnp.sum(weights, axis=-1)  17.9 us
    all_to_all x1, starting transfers between devices, split_heads(): lax.all_to_all(spread_marks, 'ctx', split_axis=1, concat_axis=0, tiled=True)  7.31 us
  transfers between devices with their start and end apart: 6, of which 5 were waited for; matrix products, arithmetic and copies ran while one was open for 36% of the time, Pallas kernels for 0%

profile of v1, /device:TPU:0, one launch (start us, length us, event | category | flops | bytes accessed | tf_op | source)
XLA Modules:
  0.0 248.5 jit_solution(6279608549576770718)
XLA Ops:
  3.1 7.3 %all-to-all-start = ((bf16[8,2,128]{2,1,0:T(2,128)(2,1)}), bf16[8,2,128]{2,1,0:T(2,128)(2,1)S(1)}, u32[]{:S(2)}, u32[]{:S(2)}) async-start(bf16[8,2,128]{2,1,0:T(2,128)(2,1)} %reshape.92), calls=%async_computation | async-start | bytes 8192 | tf_op jit(solution)/shard_map/all_to_all | solution.py:27
  10.4 1.0 stack_reshape_squeeze.6
  11.5 1.0 stack_reshape_squeeze.7
  12.9 3.9 %all-to-all-done = bf16[8,2,128]{2,1,0:T(2,128)(2,1)S(1)} async-done(((bf16[8,2,128]{2,1,0:T(2,128)(2,1)}), bf16[8,2,128]{2,1,0:T(2,128)(2,1)S(1)}, u32[]{:S(2)}, u32[]{:S(2)}) %all-to-all-start) | async-done | bytes 4128 | tf_op jit(solution)/shard_map/all_to_all | solution.py:27
  16.9 1.2 broadcast_in_dim.25
  18.0 3.6 %all-to-all-start.2 = ((bf16[256,8,2,128]{3,0,2,1:T(8,128)(2,1)}), bf16[256,8,2,128]{3,0,2,1:T(8,128)(2,1)S(1)}, u32[]{:S(2)}, u32[]{:S(2)}) async-start(bf16[256,8,2,128]{3,0,2,1:T(8,128)(2,1)} %bitcast.6), calls=%async_computation.2 | async-start | bytes 2097152 | tf_op jit(solution)/shard_map/all_to_all | solution.py:26
  21.6 3.3 %copy.50 = bf16[1,256,4096]{1,2,0:T(8,128)(2,1)S(1)} copy(bf16[1,256,4096]{2,1,0:T(8,128)(2,1)} %param.7) | data formatting | bytes 4194304 | tf_op args[0]
  24.9 2.4 copy.51
  27.3 19.0 %all-to-all-done.2 = bf16[256,8,2,128]{3,0,2,1:T(8,128)(2,1)S(1)} async-done(((bf16[256,8,2,128]{3,0,2,1:T(8,128)(2,1)}), bf16[256,8,2,128]{3,0,2,1:T(8,128)(2,1)S(1)}, u32[]{:S(2)}, u32[]{:S(2)}) %all-to-all-start.2) | async-done | bytes 1048608 | tf_op jit(solution)/shard_map/all_to_all | solution.py:26
  46.3 3.6 %all-to-all-start.1 = ((bf16[256,8,4,128]{3,0,2,1:T(8,128)(2,1)}), bf16[256,8,4,128]{3,0,2,1:T(8,128)(2,1)S(1)}, u32[]{:S(2)}, u32[]{:S(2)}) async-start(bf16[256,8,4,128]{3,0,2,1:T(8,128)(2,1)} %copy.51), calls=%async_computation.1 | async-start | bytes 4194304 | tf_op jit(solution)/shard_map/all_to_all | solution.py:36
  50.7 1.0 reshape_squeeze.11
  51.8 1.0 copy.57
  53.9 0.9 copy.67
  55.8 42.4 %all-to-all-done.1 = bf16[256,8,4,128]{3,0,2,1:T(8,128)(2,1)S(1)} async-done(((bf16[256,8,4,128]{3,0,2,1:T(8,128)(2,1)}), bf16[256,8,4,128]{3,0,2,1:T(8,128)(2,1)S(1)}, u32[]{:S(2)}, u32[]{:S(2)}) %all-to-all-start.1) | async-done | bytes 2097184 | tf_op jit(solution)/shard_map/all_to_all | solution.py:36
  98.2 3.2 %all-to-all-start.5 = ((bf16[4,2,2]{1,2,0:T(2,128)(2,1)}), bf16[4,2,2]{1,2,0:T(2,128)(2,1)S(1)}, u32[]{:S(2)}, u32[]{:S(2)}) async-start(bf16[4,2,2]{1,2,0:T(2,128)(2,1)} %copy.60), calls=%async_computation.5 | async-start | bytes 4096 | tf_op jit(solution)/shard_map/all_to_all | solution.py:112
  101.4 1.5 copy.52
  102.9 68.2 %while.11 = (s32[]{:T(128)}, bf16[4,512,4,128]{3,1,0,2:T(8,128)(2,1)}, s32[4]{0:T(128)S(1)}, bf16[2048]{0:T(1024)(128)(2,1)S(1)}, bf16[2048,1]{0,1:T(2,128)(2,1)...) while((s32[]{:T(128)}, ...), condition=%wide.region_3.4_spmd.clone, body=%wide.region_0.3_spmd.clone.sunk | while | flops 2199384576 | bytes 56684228 | solution.py:63
  104.2 1.2 fusion.52
  105.4 4.6 %bitcast_reduce_fusion.3 = (f32[4,512]{1,0:T(4,128)S(1)}, f32[512,4,2048]{2,0,1:T(8,128)S(1)}) fusion(pred[512,2048]{1,0:T(8,128)(4,1)S(1)} %fusion.52, bf16[2048,128]{1,0:T(8,128)(2,1)S(1)} %get-tuple-element.186, bf16[2048,4,128]{2,0,1:T(8,128)(2,1)} %get-tuple-element.185, s32[]{:T(128)S(6)} %select_n.39), kind=kOutput, calls=%fused_computation.2.clone.1 | convolution fusion | flops 1086322688 | bytes 18882564 | tf_op jit(solution)/shard_map/while/body/eval_jaxpr/qhe,ke->hqk/dot_general | solution.py:45
  110.0 4.5 %fusion.53 = f32[4,512]{1,0:T(4,128)S(1)} fusion(f32[512,4,2048]{2,0,1:T(8,128)S(1)} %get-tuple-element.152, f32[4,512]{1,0:T(4,128)S(1)} %get-tuple-element.153, pred[512,2048]{1,0:T(8,128)(4,1)S(1)} %fusion.52), kind=kLoop, calls=%fused_computation.5.clone.1 | loop fusion | flops 16775168 | bytes 17842176 | tf_op jit(solution)/shard_map/while/body/eval_jaxpr/reduce_sum | solution.py:54
  114.5 5.4 %fusion.54 = bf16[4,512,4,128]{3,1,0,2:T(8,128)(2,1)} fusion(bf16[4,512,4,128]{3,1,0,2:T(8,128)(2,1)} %get-tuple-element.168, s32[]{:T(128)} %get-tuple-element.167, f32[512,4,2048]{2,0,1:T(8,128)S(1)} %get-tuple-element.152, f32[4,512]{1,0:T(4,128)S(1)} %get-tuple-element.153, pred[512,2048]{1,0:T(8,128)(4,1)S(1)} %fusion.52, ...), kind=kOutput, calls=%fused_computation.14.clone.1 | convolution fusion | flops 1091043328 | bytes 18891264 | tf_op jit(solution)/shard_map/while/body/eval_jaxpr/hqk,ke->qhe/dot_general | solution.py:55
  121.3 1.2 fusion.52
  122.5 4.6 %bitcast_reduce_fusion.3 = (f32[4,512]{1,0:T(4,128)S(1)}, f32[512,4,2048]{2,0,1:T(8,128)S(1)}) fusion(pred[512,2048]{1,0:T(8,128)(4,1)S(1)} %fusion.52, bf16[2048,128]{1,0:T(8,128)(2,1)S(1)} %get-tuple-element.186, bf16[2048,4,128]{2,0,1:T(8,128)(2,1)} %get-tuple-element.185, s32[]{:T(128)S(6)} %select_n.39), kind=kOutput, calls=%fused_computation.2.clone.1 | convolution fusion | flops 1086322688 | bytes 18882564 | tf_op jit(solution)/shard_map/while/body/eval_jaxpr/qhe,ke->hqk/dot_general | solution.py:45
  127.1 4.5 %fusion.53 = f32[4,512]{1,0:T(4,128)S(1)} fusion(f32[512,4,2048]{2,0,1:T(8,128)S(1)} %get-tuple-element.152, f32[4,512]{1,0:T(4,128)S(1)} %get-tuple-element.153, pred[512,2048]{1,0:T(8,128)(4,1)S(1)} %fusion.52), kind=kLoop, calls=%fused_computation.5.clone.1 | loop fusion | flops 16775168 | bytes 17842176 | tf_op jit(solution)/shard_map/while/body/eval_jaxpr/reduce_sum | solution.py:54
  131.5 5.4 %fusion.54 = bf16[4,512,4,128]{3,1,0,2:T(8,128)(2,1)} fusion(bf16[4,512,4,128]{3,1,0,2:T(8,128)(2,1)} %get-tuple-element.168, s32[]{:T(128)} %get-tuple-element.167, f32[512,4,2048]{2,0,1:T(8,128)S(1)} %get-tuple-element.152, f32[4,512]{1,0:T(4,128)S(1)} %get-tuple-element.153, pred[512,2048]{1,0:T(8,128)(4,1)S(1)} %fusion.52, ...), kind=kOutput, calls=%fused_computation.14.clone.1 | convolution fusion | flops 1091043328 | bytes 18891264 | tf_op jit(solution)/shard_map/while/body/eval_jaxpr/hqk,ke->qhe/dot_general | solution.py:55
  138.3 1.2 fusion.52
  139.5 4.6 %bitcast_reduce_fusion.3 = (f32[4,512]{1,0:T(4,128)S(1)}, f32[512,4,2048]{2,0,1:T(8,128)S(1)}) fusion(pred[512,2048]{1,0:T(8,128)(4,1)S(1)} %fusion.52, bf16[2048,128]{1,0:T(8,128)(2,1)S(1)} %get-tuple-element.186, bf16[2048,4,128]{2,0,1:T(8,128)(2,1)} %get-tuple-element.185, s32[]{:T(128)S(6)} %select_n.39), kind=kOutput, calls=%fused_computation.2.clone.1 | convolution fusion | flops 1086322688 | bytes 18882564 | tf_op jit(solution)/shard_map/while/body/eval_jaxpr/qhe,ke->hqk/dot_general | solution.py:45
  144.1 4.5 %fusion.53 = f32[4,512]{1,0:T(4,128)S(1)} fusion(f32[512,4,2048]{2,0,1:T(8,128)S(1)} %get-tuple-element.152, f32[4,512]{1,0:T(4,128)S(1)} %get-tuple-element.153, pred[512,2048]{1,0:T(8,128)(4,1)S(1)} %fusion.52), kind=kLoop, calls=%fused_computation.5.clone.1 | loop fusion | flops 16775168 | bytes 17842176 | tf_op jit(solution)/shard_map/while/body/eval_jaxpr/reduce_sum | solution.py:54
  148.6 5.4 %fusion.54 = bf16[4,512,4,128]{3,1,0,2:T(8,128)(2,1)} fusion(bf16[4,512,4,128]{3,1,0,2:T(8,128)(2,1)} %get-tuple-element.168, s32[]{:T(128)} %get-tuple-element.167, f32[512,4,2048]{2,0,1:T(8,128)S(1)} %get-tuple-element.152, f32[4,512]{1,0:T(4,128)S(1)} %get-tuple-element.153, pred[512,2048]{1,0:T(8,128)(4,1)S(1)} %fusion.52, ...), kind=kOutput, calls=%fused_computation.14.clone.1 | convolution fusion | flops 1091043328 | bytes 18891264 | tf_op jit(solution)/shard_map/while/body/eval_jaxpr/hqk,ke->qhe/dot_general | solution.py:55
  155.4 1.2 fusion.52
  156.6 4.6 %bitcast_reduce_fusion.3 = (f32[4,512]{1,0:T(4,128)S(1)}, f32[512,4,2048]{2,0,1:T(8,128)S(1)}) fusion(pred[512,2048]{1,0:T(8,128)(4,1)S(1)} %fusion.52, bf16[2048,128]{1,0:T(8,128)(2,1)S(1)} %get-tuple-element.186, bf16[2048,4,128]{2,0,1:T(8,128)(2,1)} %get-tuple-element.185, s32[]{:T(128)S(6)} %select_n.39), kind=kOutput, calls=%fused_computation.2.clone.1 | convolution fusion | flops 1086322688 | bytes 18882564 | tf_op jit(solution)/shard_map/while/body/eval_jaxpr/qhe,ke->hqk/dot_general | solution.py:45
  161.1 4.5 %fusion.53 = f32[4,512]{1,0:T(4,128)S(1)} fusion(f32[512,4,2048]{2,0,1:T(8,128)S(1)} %get-tuple-element.152, f32[4,512]{1,0:T(4,128)S(1)} %get-tuple-element.153, pred[512,2048]{1,0:T(8,128)(4,1)S(1)} %fusion.52), kind=kLoop, calls=%fused_computation.5.clone.1 | loop fusion | flops 16775168 | bytes 17842176 | tf_op jit(solution)/shard_map/while/body/eval_jaxpr/reduce_sum | solution.py:54
  165.6 5.4 %fusion.54 = bf16[4,512,4,128]{3,1,0,2:T(8,128)(2,1)} fusion(bf16[4,512,4,128]{3,1,0,2:T(8,128)(2,1)} %get-tuple-element.168, s32[]{:T(128)} %get-tuple-element.167, f32[512,4,2048]{2,0,1:T(8,128)S(1)} %get-tuple-element.152, f32[4,512]{1,0:T(4,128)S(1)} %get-tuple-element.153, pred[512,2048]{1,0:T(8,128)(4,1)S(1)} %fusion.52, ...), kind=kOutput, calls=%fused_computation.14.clone.1 | convolution fusion | flops 1091043328 | bytes 18891264 | tf_op jit(solution)/shard_map/while/body/eval_jaxpr/hqk,ke->qhe/dot_general | solution.py:55
  171.0 1.0 fusion.39
  172.0 1.0 fusion.38
  173.0 1.0 fusion.37
  174.0 1.0 fusion.36
  175.0 1.0 fusion.35
  176.0 1.0 fusion.34
  177.0 3.5 %all-to-all-start.4 = ((bf16[4,2,2,128,128]{4,3,2,1,0:T(8,128)(2,1)}), bf16[4,2,2,128,128]{4,3,2,1,0:T(8,128)(2,1)S(1)}, u32[]{:S(2)}, u32[]{:S(2)}) async-start(bf16[4,2,2,128,128]{4,3,2,1,0:T(8,128)(2,1)} %bitcast.50), calls=%async_computation.4 | async-start | bytes 1048576 | tf_op jit(solution)/shard_map/all_to_all | solution.py:111
  180.5 1.0 fusion.33
  181.5 1.0 fusion.32
  182.5 1.3 copy-done
  183.8 5.5 %all-to-all-done.4 = bf16[4,2,2,128,128]{4,3,2,1,0:T(8,128)(2,1)S(1)} async-done(((bf16[4,2,2,128,128]{4,3,2,1,0:T(8,128)(2,1)}), bf16[4,2,2,128,128]{4,3,2,1,0:T(8,128)(2,1)S(1)}, u32[]{:S(2)}, u32[]{:S(2)}) %all-to-all-start.4) | async-done | bytes 524320 | tf_op jit(solution)/shard_map/all_to_all | solution.py:111
  189.3 3.6 %all-to-all-start.3 = ((bf16[8,256,1,4,128]{4,1,3,2,0:T(8,128)(2,1)}), bf16[8,256,1,4,128]{4,1,3,2,0:T(8,128)(2,1)S(1)}, u32[]{:S(2)}, u32[]{:S(2)}) async-start(bf16[8,256,1,4,128]{4,1,3,2,0:T(8,128)(2,1)} %copy-done), calls=%async_computation.3 | async-start | bytes 4194304 | tf_op jit(solution)/shard_map/all_to_all | solution.py:68
  193.5 47.5 %all-to-all-done.3 = bf16[8,256,1,4,128]{4,1,3,2,0:T(8,128)(2,1)S(1)} async-done(((bf16[8,256,1,4,128]{4,1,3,2,0:T(8,128)(2,1)}), bf16[8,256,1,4,128]{4,1,3,2,0:T(8,128)(2,1)S(1)}, u32[]{:S(2)}, u32[]{:S(2)}) %all-to-all-start.3) | async-done | bytes 2097184 | tf_op jit(solution)/shard_map/all_to_all | solution.py:68
  241.0 2.6 %copy.56 = bf16[256,8,1,4,128]{0,4,3,1,2:T(8,128)(2,1)} copy(bf16[256,8,1,4,128]{4,0,3,2,1:T(8,128)(2,1)S(1)} %bitcast.141) | data formatting | bytes 4194304 | tf_op jit(solution)/shard_map/reshape | solution.py:67
  243.6 4.1 %copy.62 = bf16[1,256,4096]{2,1,0:T(8,128)(2,1)} copy(bf16[1,256,4096]{1,2,0:T(8,128)(2,1)} %bitcast.142) | data formatting | bytes 4194304
  (51 shorter events, 10.1 us)
Async XLA Ops:
  3.1 13.7 %all-to-all-start = ((bf16[8,2,128]{2,1,0:T(2,128)(2,1)}), bf16[8,2,128]{2,1,0:T(2,128)(2,1)S(1)}, u32[]{:S(2)}, u32[]{:S(2)}) async-start(bf16[8,2,128]{2,1,0:T(2,128)(2,1)} %reshape.92), calls=%async_computation | async-start | bytes 8192 | tf_op jit(solution)/shard_map/all_to_all | solution.py:27
  18.0 28.3 %all-to-all-start.2 = ((bf16[256,8,2,128]{3,0,2,1:T(8,128)(2,1)}), bf16[256,8,2,128]{3,0,2,1:T(8,128)(2,1)S(1)}, u32[]{:S(2)}, u32[]{:S(2)}) async-start(bf16[256,8,2,128]{3,0,2,1:T(8,128)(2,1)} %bitcast.6), calls=%async_computation.2 | async-start | bytes 2097152 | tf_op jit(solution)/shard_map/all_to_all | solution.py:26
  27.3 22.7 %copy-start.1 = (bf16[1,256,512]{2,1,0:T(8,128)(2,1)S(1)}, bf16[1,256,512]{2,1,0:T(8,128)(2,1)}, u32[]{:S(2)}) copy-start(bf16[1,256,512]{2,1,0:T(8,128)(2,1)} %param.8) | copy-start | bytes 786436
  46.3 51.9 %all-to-all-start.1 = ((bf16[256,8,4,128]{3,0,2,1:T(8,128)(2,1)}), bf16[256,8,4,128]{3,0,2,1:T(8,128)(2,1)S(1)}, u32[]{:S(2)}, u32[]{:S(2)}) async-start(bf16[256,8,4,128]{3,0,2,1:T(8,128)(2,1)} %copy.51), calls=%async_computation.1 | async-start | bytes 4194304 | tf_op jit(solution)/shard_map/all_to_all | solution.py:36
  50.7 2.5 %copy-start.2 = (s32[1,8,1]{1,2,0:T(1,128)S(1)}, s32[1,8,1]{1,2,0:T(1,128)}, u32[]{:S(2)}) copy-start(s32[1,8,1]{1,2,0:T(1,128)} %param.11) | copy-start | bytes 100
  98.2 78.8 %all-to-all-start.5 = ((bf16[4,2,2]{1,2,0:T(2,128)(2,1)}), bf16[4,2,2]{1,2,0:T(2,128)(2,1)S(1)}, u32[]{:S(2)}, u32[]{:S(2)}) async-start(bf16[4,2,2]{1,2,0:T(2,128)(2,1)} %copy.60), calls=%async_computation.5 | async-start | bytes 4096 | tf_op jit(solution)/shard_map/all_to_all | solution.py:112
  177.0 12.3 %all-to-all-start.4 = ((bf16[4,2,2,128,128]{4,3,2,1,0:T(8,128)(2,1)}), bf16[4,2,2,128,128]{4,3,2,1,0:T(8,128)(2,1)S(1)}, u32[]{:S(2)}, u32[]{:S(2)}) async-start(bf16[4,2,2,128,128]{4,3,2,1,0:T(8,128)(2,1)} %bitcast.50), calls=%async_computation.4 | async-start | bytes 1048576 | tf_op jit(solution)/shard_map/all_to_all | solution.py:111
  182.5 1.3 copy-start
  189.3 51.8 %all-to-all-start.3 = ((bf16[8,256,1,4,128]{4,1,3,2,0:T(8,128)(2,1)}), bf16[8,256,1,4,128]{4,1,3,2,0:T(8,128)(2,1)S(1)}, u32[]{:S(2)}, u32[]{:S(2)}) async-start(bf16[8,256,1,4,128]{4,1,3,2,0:T(8,128)(2,1)} %copy-done), calls=%async_computation.3 | async-start | bytes 4194304 | tf_op jit(solution)/shard_map/all_to_all | solution.py:68
